TPU v7x, 1024 devices: a whole 4x4x32 slice. The times are simulated.
1024 devices in a mesh: row: 64 (over z, y_hi), col: 16 (over y_lo, x, core).
Axes of the slice: x: 4, y: 4 (y_hi: 2, y_lo: 2; y = y_hi * 2 + y_lo), z: 32, core: 2. Of those that a mesh axis runs over, the one named last changes fastest.
Arguments:
- valence_pairs: bfloat16 [128, 128, 1024], P('row', 'col'), may hold values from -0.09375 to 0.09375
- conduction_pairs: bfloat16 [192, 192, 1024], P('row', 'col'), may hold values from -0.09375 to 0.09375
- screening: bfloat16 [1024, 1024], replicated, may hold values from -0.0390625 to 1.5
- valence_energy: float32 [128], P('col'), may hold values from -2 to 0
- conduction_energy: float32 [192], P('row'), may hold values from 3 to 6
- vectors: bfloat16 [192, 128, 128], P('row', 'col'), may hold values from -6 to 6
Outputs:
- first_step: bfloat16 [192, 128, 128], P('row', 'col')
- filtered: float32 [192, 128, 128], P('row', 'col')
All inputs are finite; a program needn't handle non-finite values.
Results may differ from a plain program's by a relative error of at most 0.0043.
Values may be sent and summed in bfloat16 or wider, within the bound.
A program may use at most 64 MiB of HBM per device.

v0:
```python
import jax
import jax.numpy as jnp
from jax import lax
from jax.sharding import PartitionSpec as P

shift_center = 5.5
half_width = 3.0


def screen_rows(portion, screening):
    aux_width = portion.shape[2]
    flattened = portion.reshape(-1, aux_width)
    product = jnp.dot(flattened, screening, preferred_element_type=jnp.float32)
    return product.astype(jnp.bfloat16).reshape(portion.shape)


def on_device(
    valence_pairs, conduction_pairs, screening, valence_energy, conduction_energy, vectors
):
    screened = lax.all_gather(screen_rows(valence_pairs, screening), "row", axis=0, tiled=True)
    kernel_tile = jnp.einsum(
        "vwp,cdp->cvwd",
        screened,
        lax.all_gather(conduction_pairs, "col", axis=1, tiled=True),
        preferred_element_type=jnp.float32,
    ).astype(jnp.bfloat16)
    energy_gaps = (conduction_energy[:, None] - valence_energy[None, :] - shift_center)[:, :, None]

    def operator(current):
        partial_sum = jnp.einsum(
            "cvwd,dwk->cvk",
            kernel_tile,
            lax.all_gather(current, "row", axis=0, tiled=True),
            preferred_element_type=jnp.float32,
        )
        coupled = lax.psum_scatter(partial_sum, "col", scatter_dimension=1, tiled=True)
        return (energy_gaps * current.astype(jnp.float32) - coupled) / half_width

    first_step = operator(vectors).astype(jnp.bfloat16)
    filtered = 2.0 * operator(first_step) - vectors.astype(jnp.float32)
    return (first_step, filtered)


def solution(mesh):
    return jax.shard_map(
        on_device,
        mesh=mesh,
        in_specs=(
            P("row", "col", None),
            P("row", "col", None),
            P(),
            P("col"),
            P("row"),
            P("row", "col", None),
        ),
        out_specs=(P("row", "col", None), P("row", "col", None)),
        check_vma=False,
    )
```

profile of v0, /device:TPU:1, one launch (start us, length us, event | category | flops | bytes accessed | tf_op | source)
XLA Modules:
  0.0 657.8 jit_solution(13222634714689553126)
XLA Ops:
  7.2 0.0 copy-start
  7.2 0.0 copy-start.1
  7.2 0.0 all-gather.5.cloned.1.call-start
  7.2 1.7 copy.13
  9.0 0.0 all-gather.5.cloned.1.call-update
  9.0 0.0 all-gather.3.cloned.1.call-start
  9.0 0.0 copy-done
  9.1 1.8 fusion.10
  10.8 0.0 all-gather.3.cloned.1.call-update
  10.8 0.0 reduce-scatter.3.cloned.1.call-start
  10.9 0.0 copy-done.1
  10.9 135.1 %all_gather.14 = bf16[192,8,128]{2,1,0:T(8,128)(2,1)S(1)} all-gather(bf16[3,8,128]{2,1,0:T(8,128)(2,1)S(1)} %copy-done.1), channel_id=1, replica_groups=mesh['row'=64,'col'=16] {'row'}, dimensions={0}, use_global_device_ids=true | all-gather | bytes 399360 | tf_op jit(solution)/shard_map/all_gather | solution.py:33
  146.0 186.6 %all-gather.3.cloned.1.call-done = bf16[128,8,1024]{2,1,0:T(8,128)(2,1)} async-done(((bf16[2,8,1024]{2,1,0:T(8,128)(2,1)}), bf16[128,8,1024]{2,1,0:T(8,128)(2,1)}) %all-gather.3.cloned.1.call-update) | async-done | bytes 2097168 | tf_op jit(solution)/shard_map/all_gather | solution.py:20
  332.6 6.1 fusion.5
  338.6 0.0 copy-start.5
  338.7 0.0 copy-start.3
  338.7 0.0 copy-start.4
  338.7 1.0 copy-done.5
  339.7 1.2 convolution_bitcast_fusion.1
  340.9 0.0 reduce-scatter.3.cloned.1.call-update
  340.9 0.0 reduce-scatter.5.cloned.1.call-start
  341.0 0.0 copy-done.3
  341.0 0.0 copy-done.4
  341.0 0.1 subtract_add_fusion
  341.1 85.5 %reduce-scatter.3.cloned.1.call-done = f32[3,8,128]{2,1,0:T(8,128)} async-done(((f32[3,128,128]{2,1,0:T(8,128)}), f32[3,8,128]{2,1,0:T(8,128)}) %reduce-scatter.3.cloned.1.call-update) | async-done | bytes 12304 | tf_op jit(solution)/shard_map/reduce_scatter | solution.py:36
  426.6 0.8 fusion.16
  427.4 119.7 %all_gather.15 = bf16[192,8,128]{2,1,0:T(8,128)(2,1)S(1)} all-gather(bf16[3,8,128]{2,1,0:T(8,128)(2,1)S(1)} %fusion.16), channel_id=1, replica_groups=mesh['row'=64,'col'=16] {'row'}, dimensions={0}, use_global_device_ids=true | all-gather | bytes 399360 | tf_op jit(solution)/shard_map/all_gather | solution.py:33
  547.1 2.5 convolution_bitcast_fusion
  549.6 0.0 reduce-scatter.5.cloned.1.call-update
  549.6 100.3 %reduce-scatter.5.cloned.1.call-done = f32[3,8,128]{2,1,0:T(8,128)} async-done(((f32[3,128,128]{2,1,0:T(8,128)}), f32[3,8,128]{2,1,0:T(8,128)}) %reduce-scatter.5.cloned.1.call-update) | async-done | bytes 12304 | tf_op jit(solution)/shard_map/reduce_scatter | solution.py:36
  649.9 1.4 convert_subtract_fusion
  651.2 0.0 copy-done.2
  (2 shorter events, 0.0 us)
Async XLA Ops:
  7.2 1.9 copy-start
  7.2 3.7 copy-start.1
  7.2 138.8 %all-gather.5.cloned.1.call-start = ((), (), s32[]{:S(2)}) async-start(), calls=%async_computation.3 | async-start | bytes 1671168 | tf_op jit(solution)/shard_map/all_gather | solution.py:24
  9.0 323.6 %all-gather.3.cloned.1.call-start = ((), (), s32[]{:S(2)}) async-start(), calls=%async_computation.2 | async-start | bytes 2129920 | tf_op jit(solution)/shard_map/all_gather | solution.py:20
  10.8 415.8 %reduce-scatter.3.cloned.1.call-start = ((), (), s32[]{:S(2)}) async-start(), calls=%async_computation.4 | async-start | bytes 208896 | tf_op jit(solution)/shard_map/reduce_scatter | solution.py:36
  338.6 1.0 copy-start.5
  338.7 2.3 copy-start.3
  338.7 2.3 copy-start.4
  340.9 308.9 %reduce-scatter.5.cloned.1.call-start = ((), (), s32[]{:S(2)}) async-start(), calls=%async_computation.5 | async-start | bytes 208896 | tf_op jit(solution)/shard_map/reduce_scatter | solution.py:36
  427.4 223.9 %copy-start.2 = (bf16[3,8,128]{2,1,0:T(8,128)(2,1)}, bf16[3,8,128]{2,1,0:T(8,128)(2,1)S(1)}, u32[]{:S(2)}) copy-start(bf16[3,8,128]{2,1,0:T(8,128)(2,1)S(1)} %fusion.16) | copy-start | bytes 18436
Sparse Core Ops, SparseCore 0:
  10.7 59.9 all-gather.4
  75.0 257.5 all-gather.2
  341.0 85.5 reduce-scatter.2
  549.7 100.0 reduce-scatter.4
where the time goes:
time: 658 us
  waiting for transfers between devices  372 us (57%)
  blocking collectives  255 us (39%)
  between operations  13.8 us (2%)
  matrix products  11.5 us (2%)
    all_gather x2, blocking collectives, operator(): lax.all_gather(current, 'row', axis=0, tiled=True)  255 us
    all_gather x1, waiting for transfers between devices, on_device(): lax.all_gather(screen_rows(valence_pairs, screening), 'row', axis=0, tile...  187 us
    reduce_scatter x2, waiting for transfers between devices, operator(): lax.psum_scatter(partial_sum, 'col', scatter_dimension=1, tiled=True)  186 us
  transfers between devices with their start and end apart: 4, of which 3 were waited for; matrix products, arithmetic and copies ran while one was open for 0% of the time, Pallas kernels for 0%

commit v1 on v0

v1 whole, which is shorter than its diff:
```python
import jax
import jax.numpy as jnp
from jax import lax
from jax.experimental import pallas as pl
from jax.experimental.pallas import tpu as pltpu
from jax.sharding import PartitionSpec as P

shift_center = 5.5
half_width = 3.0

NZ = 32
NQ = 16
NPLANE = 32
FAR = (16, 12, 20, 8, 24, 4, 28)
NEAR = (1, 31, 2)
GREETED = (1, 2, 4, 8, 12, 16, 20, 24, 28, 30, 31)
MESH = pl.DeviceIdType.MESH


def body(
    v_ref, c_ref, screening_ref, gaps_ref, u_ref,
    first_ref, filtered_ref,
    v_both, screen_half, s_ring, s_wide, s_rows, c_all, k_tile,
    u_one, u_two, u_wide, u_rows, y_part, y_two, r_one, r_two,
    local_sem, v_sem, c_send, c_recv, right_send, right_recv, left_send, left_recv,
    gather_send, gather_recv, sum_send, sum_recv,
):
    row = lax.axis_index("row")
    q = lax.axis_index("col")
    z = row // 2
    y = row % 2
    me = y * NQ + q
    z_class = z % 4
    z_step = z // 4

    def plane_id(i):
        p = (me + i) % NPLANE
        return p // NQ, p % NQ

    def z_id(distance):
        return (((z + distance) % NZ) * 2 + y, q)

    barrier = pltpu.get_barrier_semaphore()

    @pl.loop(1, NPLANE)
    def _(i):
        ty, tq = plane_id(i)
        pl.semaphore_signal(barrier, inc=1, device_id=(z * 2 + ty, tq), device_id_type=MESH)

    for distance in GREETED:
        pl.semaphore_signal(barrier, inc=1, device_id=z_id(distance), device_id_type=MESH)

    screen_copy = pltpu.make_async_copy(
        screening_ref.at[:, pl.ds(pl.multiple_of(y * 512, 512), 512)], screen_half, local_sem.at[0]
    )
    screen_copy.start()
    own_c = pltpu.make_async_copy(
        c_ref.at[y],
        c_all.at[pl.ds(y * 3, 3), pl.ds(pl.multiple_of(q * 16, 16), 16), :],
        local_sem.at[1],
    )
    own_c.start()
    u_wide[...] = jnp.zeros_like(u_wide)
    u_one[z_class, z_step, y] = u_ref[...]
    pl.semaphore_wait(barrier, NPLANE - 1 + len(GREETED))

    partner = ((z * 2 + 1 - y), q)
    v_copy = pltpu.make_async_remote_copy(
        src_ref=v_ref, dst_ref=v_both.at[y], send_sem=v_sem.at[0], recv_sem=v_sem.at[1],
        device_id=partner, device_id_type=MESH,
    )
    v_copy.start()

    def pair_copy(buf, op):
        return pltpu.make_async_remote_copy(
            src_ref=buf.at[z_class, z_step, y], dst_ref=buf.at[z_class, z_step, y],
            send_sem=gather_send.at[op, 0], recv_sem=gather_recv.at[op, 0],
            device_id=partner, device_id_type=MESH,
        )

    def far_copy(buf, op, n):
        return pltpu.make_async_remote_copy(
            src_ref=buf.at[z_class, z_step], dst_ref=buf.at[z_class, z_step],
            send_sem=gather_send.at[op, 1 + n], recv_sem=gather_recv.at[op, 1 + n],
            device_id=z_id(FAR[n]), device_id_type=MESH,
        )

    def near_copy(buf, op, n):
        return pltpu.make_async_remote_copy(
            src_ref=buf.at[z_class], dst_ref=buf.at[z_class],
            send_sem=gather_send.at[op, 8 + n], recv_sem=gather_recv.at[op, 8 + n],
            device_id=z_id(NEAR[n]), device_id_type=MESH,
        )

    pair_copy(u_one, 0).start()

    def c_copy(i):
        ty, tq = plane_id(i)
        return pltpu.make_async_remote_copy(
            src_ref=c_ref.at[ty],
            dst_ref=c_all.at[pl.ds(y * 3, 3), pl.ds(pl.multiple_of(q * 16, 16), 16), :],
            send_sem=c_send.at[i], recv_sem=c_recv.at[i],
            device_id=(z * 2 + ty, tq), device_id_type=MESH,
        )

    v_both[y] = v_ref[...]

    @pl.loop(1, NPLANE)
    def _(i):
        c_copy(i).start()

    screen_copy.wait()
    v_copy.wait()
    raw = v_both[...].astype(jnp.float32).reshape(32, 1024).astype(jnp.bfloat16)
    s_ring[z] = jnp.dot(raw, screen_half[...], preferred_element_type=jnp.float32).astype(jnp.bfloat16)

    def right_copy(s):
        block = (z + NZ - s) % NZ
        return pltpu.make_async_remote_copy(
            src_ref=s_ring.at[block], dst_ref=s_ring.at[block],
            send_sem=right_send.at[s], recv_sem=right_recv.at[s],
            device_id=z_id(1), device_id_type=MESH,
        )

    def left_copy(s):
        block = (z + s) % NZ
        return pltpu.make_async_remote_copy(
            src_ref=s_ring.at[block], dst_ref=s_ring.at[block],
            send_sem=left_send.at[s], recv_sem=left_recv.at[s],
            device_id=z_id(NZ - 1), device_id_type=MESH,
        )

    def widen(block):
        rows = s_ring[block].astype(jnp.float32)
        for j in range(4):
            s_wide[j, pl.ds(pl.multiple_of(block * 32, 32), 32), :] = rows[:, j * 128:(j + 1) * 128]

    def ring_step(s):
        right_copy(s).start()
        left_copy(s).start()
        widen((z + NZ - s) % NZ)
        widen((z + s) % NZ)
        right_copy(s).wait_recv()
        left_copy(s).wait_recv()

    right_copy(0).start()
    left_copy(0).start()
    pair_copy(u_one, 0).wait()
    for n in range(len(FAR)):
        far_copy(u_one, 0, n).start()
    widen(z)
    right_copy(0).wait_recv()
    left_copy(0).wait_recv()

    @pl.loop(1, 9)
    def _(s):
        ring_step(s)

    for n in range(len(FAR)):
        far_copy(u_one, 0, n).wait()
    for n in range(len(NEAR)):
        near_copy(u_one, 0, n).start()

    @pl.loop(9, 15)
    def _(s):
        ring_step(s)

    right_copy(15).start()
    widen((z + 17) % NZ)
    widen((z + 15) % NZ)
    right_copy(15).wait_recv()
    widen((z + 16) % NZ)

    @pl.loop(0, 8)
    def _(w):
        for j in range(4):
            s_rows[w, :, j * 128:(j + 1) * 128] = s_wide[j, pl.ds(w, 128, stride=8), :].astype(jnp.bfloat16)

    own_c.wait()

    @pl.loop(1, NPLANE)
    def _(i):
        c_copy(i).wait()

    @pl.loop(0, 6)
    def _(c):
        conduction = c_all[c]
        for w in range(8):
            k_tile[c, :, w * 256:(w + 1) * 256] = lax.dot_general(
                s_rows[w], conduction, (((1,), (1,)), ((), ())), preferred_element_type=jnp.float32
            ).astype(jnp.bfloat16)

    for n in range(len(NEAR)):
        near_copy(u_one, 0, n).wait()

    def products(buf, part):
        for za in range(4):
            for zq in range(8):
                start = (zq * 2 + za // 2) * 128 + (za % 2) * 48
                for half in range(2):
                    u_wide[start + half * 24:start + half * 24 + 24, :] = (
                        buf[za, zq, half].astype(jnp.float32).reshape(24, 128)
                    )

        for w in range(8):
            u_rows[w * 256:(w + 1) * 256, :] = u_wide[pl.ds(w, 256, stride=8), :].astype(jnp.bfloat16)

        @pl.loop(0, 6)
        def _(c):
            part[c] = jnp.dot(k_tile[c], u_rows[...], preferred_element_type=jnp.float32)

    def sum_copy(part, landing, op, i):
        ty, tq = plane_id(i)
        return pltpu.make_async_remote_copy(
            src_ref=part.at[pl.ds(ty * 3, 3), pl.ds(pl.multiple_of(tq * 8, 8), 8), :],
            dst_ref=landing.at[i],
            send_sem=sum_send.at[op, i], recv_sem=sum_recv.at[op, i],
            device_id=(z * 2 + ty, tq), device_id_type=MESH,
        )

    def reduced(part, landing, op):
        @pl.loop(1, NPLANE)
        def _(i):
            sum_copy(part, landing, op, i).start()

        landing[0] = part[pl.ds(y * 3, 3), pl.ds(pl.multiple_of(q * 8, 8), 8), :]

        @pl.loop(1, NPLANE)
        def _(i):
            sum_copy(part, landing, op, i).wait()

        return jnp.sum(landing[...], axis=0)

    products(u_one, y_part)
    start = u_ref[...].astype(jnp.float32)
    first = ((gaps_ref[...] * start - reduced(y_part, r_one, 0)) / half_width).astype(jnp.bfloat16)
    u_two[z_class, z_step, y] = first
    first_ref[...] = first

    pair_copy(u_two, 1).start()
    pair_copy(u_two, 1).wait()
    for n in range(len(FAR)):
        far_copy(u_two, 1, n).start()
    for n in range(len(FAR)):
        far_copy(u_two, 1, n).wait()
    for n in range(len(NEAR)):
        near_copy(u_two, 1, n).start()
    for n in range(len(NEAR)):
        near_copy(u_two, 1, n).wait()

    products(u_two, y_two)
    second = (gaps_ref[...] * first.astype(jnp.float32) - reduced(y_two, r_two, 1)) / half_width
    filtered_ref[...] = 2.0 * second - start

    @pl.loop(0, 15)
    def _(s):
        right_copy(s).wait_send()
        left_copy(s).wait_send()

    right_copy(15).wait_send()


def on_device(
    valence_pairs, conduction_pairs, screening, valence_energy, conduction_energy, vectors
):
    gaps = (conduction_energy[:, None] - valence_energy[None, :] - shift_center)[:, :, None]
    gaps = jnp.broadcast_to(gaps, vectors.shape)
    padded = jnp.pad(conduction_pairs, ((0, 0), (0, 4), (0, 0)))
    halves = jnp.transpose(padded.reshape(3, 16, 2, 512), (2, 0, 1, 3))
    in_vmem = pl.BlockSpec(memory_space=pltpu.VMEM)
    bf16, f32 = jnp.bfloat16, jnp.float32
    dma = pltpu.SemaphoreType.DMA
    return pl.pallas_call(
        body,
        out_shape=(
            jax.ShapeDtypeStruct(vectors.shape, bf16),
            jax.ShapeDtypeStruct(vectors.shape, f32),
        ),
        in_specs=[in_vmem, in_vmem, pl.BlockSpec(memory_space=pl.ANY), in_vmem, in_vmem],
        out_specs=(in_vmem, in_vmem),
        scratch_shapes=[
            pltpu.VMEM((2, 2, 8, 1024), bf16),
            pltpu.VMEM((1024, 512), bf16),
            pltpu.VMEM((NZ, 32, 512), bf16),
            pltpu.VMEM((4, 1024, 128), f32),
            pltpu.VMEM((8, 128, 512), bf16),
            pltpu.VMEM((6, 256, 512), bf16),
            pltpu.VMEM((6, 128, 2048), bf16),
            pltpu.VMEM((4, 8, 2, 3, 8, 128), bf16),
            pltpu.VMEM((4, 8, 2, 3, 8, 128), bf16),
            pltpu.VMEM((2048, 128), f32),
            pltpu.VMEM((2048, 128), bf16),
            pltpu.VMEM((6, 128, 128), f32),
            pltpu.VMEM((6, 128, 128), f32),
            pltpu.VMEM((NPLANE, 3, 8, 128), f32),
            pltpu.VMEM((NPLANE, 3, 8, 128), f32),
            dma((2,)),
            dma((2,)),
            dma((NPLANE,)),
            dma((NPLANE,)),
            dma((16,)),
            dma((16,)),
            dma((16,)),
            dma((16,)),
            dma((2, 11)),
            dma((2, 11)),
            dma((2, NPLANE)),
            dma((2, NPLANE)),
        ],
        compiler_params=pltpu.CompilerParams(collective_id=0, has_side_effects=True),
    )(valence_pairs, halves, screening, gaps, vectors)


def solution(mesh):
    return jax.shard_map(
        on_device,
        mesh=mesh,
        in_specs=(
            P("row", "col", None),
            P("row", "col", None),
            P(),
            P("col"),
            P("row"),
            P("row", "col", None),
        ),
        out_specs=(P("row", "col", None), P("row", "col", None)),
        check_vma=False,
    )
```

time: 658 us -> 163 us (0.25)
  waiting for transfers between devices: 372 us -> 0 us
  blocking collectives: 255 us -> 0 us
  Pallas kernels: 0 us -> 156 us
  between operations: 13.8 us -> 0.64 us
  matrix products: 11.5 us -> 0 us
    all_gather x2 -> x0, blocking collectives: 255 us -> none  [operator(): lax.all_gather(current, 'row', axis=0, tiled=True)]
    all_gather x2 -> x0, waiting for transfers between devices: 187 us -> none  [the longest x1 187 us: on_device(): lax.all_gather(screen_rows(valence_pairs, screening), 'row', axis=0, tile...]
    reduce_scatter x2 -> x0, waiting for transfers between devices: 186 us -> none  [operator(): lax.psum_scatter(partial_sum, 'col', scatter_dimension=1, tiled=True)]
    pallas_call x0 -> x1, Pallas kernels: none -> 156 us  [on_device(): pl.pallas_call(body, out_shape=(jax.ShapeDtypeStruct(vectors.shape, bf16)...]
    dot_general x4 -> x0, matrix products: 11.5 us -> none  [the longest x1 6.09 us: on_device(): jnp.einsum('vwp,cdp->cvwd', screened, lax.all_gather(conduction_pairs, 'c...]
  transfers between devices with their start and end apart: 4 -> 0, of which waited for: 3 -> 0; matrix products, arithmetic and copies ran while one was open for 0% -> 0% of each run, Pallas kernels for 0% -> 0%
where the time goes in v1:
time: 163 us; the launch traced here: 162 us
  Pallas kernels  156 us (96%)
  local copies, waits for them, and re-layouts  4.82 us (3%)
    pallas_call x1, Pallas kernels, on_device(): pl.pallas_call(body, out_shape=(jax.ShapeDtypeStruct(vectors.shape, bf16)...  156 us

profile of v1, /device:TPU:1, one launch (start us, length us, event | category | flops | bytes accessed | tf_op | source)
XLA Modules:
  0.0 162.4 jit_solution(10986775612466036000)
XLA Ops:
  0.6 0.9 pad.4
  1.5 0.6 copy.11
  2.2 0.7 subtract_add_fusion
  2.9 0.7 broadcast_in_dim.2.gaps_ref
  3.6 156.2 %shard_map.77 = (bf16[3,8,128]{2,1,0:T(8,128)(2,1)}, f32[3,8,128]{2,1,0:T(8,128)}) custom-call(bf16[2,8,1024]{2,1,0:T(8,128)(2,1)} %v_ref.1, bf16[2,3,16,512]{3,2,1,0:T(8,128)(2,1)} %bitcast.7, bf16[1024,1024]{1,0:T(8,128)(2,1)} %screening_ref.1, f32[3,8,128]{2,1,0:T(8,128)} %broadcast_in_dim.2.gaps_ref, bf16[3,8,128]{2,1,0:T(8,128)(2,1)} %u_ref.1), custom_call_target="tpu_custom_call" | custom-call | tf_op jit(solution)/shard_map/pallas_call | solution.py:273
  159.8 1.3 copy.14
  161.1 1.3 copy.15

commit v2 on v1

v2 whole, which is shorter than its diff:
```python
import jax
import jax.numpy as jnp
from jax import lax
from jax.experimental import pallas as pl
from jax.experimental.pallas import tpu as pltpu
from jax.sharding import PartitionSpec as P

shift_center = 5.5
half_width = 3.0

NZ = 32
NQ = 16
NPLANE = 32
SEEDS = (0, 24, 8, 16)
SPREAD = (4, 3, 29, 2, 30, 1, 31)
GREETED = (1, 2, 3, 4, 8, 24, 28, 29, 30, 31)
MESH = pl.DeviceIdType.MESH


def body(
    v_ref, c_ref, screening_ref, gaps_ref, u_ref,
    first_ref, filtered_ref,
    screen_own, screen_other, s_pair, s_ring, s_wide, s_rows, c_all, k_tile,
    u_one, u_two, u_wide, u_rows, y_part, y_two, r_one, r_two,
    local_sem, v_sem, c_send, c_recv, far_send, far_recv, ring_send, ring_recv,
    gather_send, gather_recv, sum_send, sum_recv,
):
    row = lax.axis_index("row")
    q = lax.axis_index("col")
    z = row // 2
    y = row % 2
    me = y * NQ + q

    def plane_id(i):
        p = (me + i) % NPLANE
        return p // NQ, p % NQ

    def z_id(distance):
        return (((z + distance) % NZ) * 2 + y, q)

    def block_at(distance):
        return (z + distance) % NZ

    barrier = pltpu.get_barrier_semaphore()

    for distance in GREETED:
        pl.semaphore_signal(barrier, inc=1, device_id=z_id(distance), device_id_type=MESH)

    @pl.loop(1, NPLANE)
    def _(i):
        ty, tq = plane_id(i)
        pl.semaphore_signal(barrier, inc=1, device_id=(z * 2 + ty, tq), device_id_type=MESH)

    def screen_copy(half, buf, n):
        return pltpu.make_async_copy(
            screening_ref.at[:, pl.ds(pl.multiple_of(half * 512, 512), 512)], buf, local_sem.at[n]
        )

    screen_copy(1 - y, screen_other, 0).start()
    screen_copy(y, screen_own, 1).start()
    own_c = pltpu.make_async_copy(
        c_ref.at[y],
        c_all.at[pl.ds(y * 3, 3), pl.ds(pl.multiple_of(q * 16, 16), 16), :],
        local_sem.at[2],
    )
    own_c.start()
    u_wide[...] = jnp.zeros_like(u_wide)
    u_one[z, y] = u_ref[...]

    raw = v_ref[...].astype(jnp.float32).reshape(16, 1024).astype(jnp.bfloat16)
    own_rows = pl.ds(pl.multiple_of(y * 16, 16), 16)
    screen_copy(1 - y, screen_other, 0).wait()
    s_pair[...] = jnp.dot(raw, screen_other[...], preferred_element_type=jnp.float32).astype(jnp.bfloat16)
    screen_copy(y, screen_own, 1).wait()
    s_ring[z, own_rows, :] = jnp.dot(raw, screen_own[...], preferred_element_type=jnp.float32).astype(
        jnp.bfloat16
    )
    pl.semaphore_wait(barrier, NPLANE - 1 + len(GREETED))

    partner = ((z * 2 + 1 - y), q)
    s_copy = pltpu.make_async_remote_copy(
        src_ref=s_pair, dst_ref=s_ring.at[z, own_rows, :], send_sem=v_sem.at[0], recv_sem=v_sem.at[1],
        device_id=partner, device_id_type=MESH,
    )
    s_copy.start()

    def pair_copy(buf, op):
        return pltpu.make_async_remote_copy(
            src_ref=buf.at[z, y], dst_ref=buf.at[z, y],
            send_sem=gather_send.at[op, 0], recv_sem=gather_recv.at[op, 0],
            device_id=partner, device_id_type=MESH,
        )

    def far_copy(buf, op, n):
        return pltpu.make_async_remote_copy(
            src_ref=buf.at[z], dst_ref=buf.at[z],
            send_sem=gather_send.at[op, 1 + n], recv_sem=gather_recv.at[op, 1 + n],
            device_id=z_id((8, 24)[n]), device_id_type=MESH,
        )

    def farther_copy(buf, op, n):
        block = block_at((24, 8)[n])
        return pltpu.make_async_remote_copy(
            src_ref=buf.at[block, n], dst_ref=buf.at[block, n],
            send_sem=gather_send.at[op, 3 + n], recv_sem=gather_recv.at[op, 3 + n],
            device_id=z_id((8, 24)[n]), device_id_type=MESH,
        )

    def spread_copy(buf, op, k, n):
        block = block_at(SEEDS[k])
        slot = 5 + k * len(SPREAD) + n
        return pltpu.make_async_remote_copy(
            src_ref=buf.at[block], dst_ref=buf.at[block],
            send_sem=gather_send.at[op, slot], recv_sem=gather_recv.at[op, slot],
            device_id=z_id(SPREAD[n]), device_id_type=MESH,
        )

    def spread(buf, op, k):
        for n in range(len(SPREAD)):
            spread_copy(buf, op, k, n).start()

    def gather_opened(buf, op):
        pair_copy(buf, op).wait()
        for n in range(2):
            far_copy(buf, op, n).start()
        spread(buf, op, 0)

    def gather_passed(buf, op):
        for n in range(2):
            far_copy(buf, op, n).wait_recv()
            farther_copy(buf, op, n).start()
        for k in (1, 2):
            spread(buf, op, k)

    def gather_closed(buf, op):
        for n in range(2):
            farther_copy(buf, op, n).wait_recv()
        spread(buf, op, 3)

    def gather_finished(buf, op):
        for k in range(4):
            for n in range(len(SPREAD)):
                spread_copy(buf, op, k, n).wait()
        for n in range(2):
            far_copy(buf, op, n).wait_send()
            farther_copy(buf, op, n).wait_send()

    pair_copy(u_one, 0).start()

    def c_copy(i):
        ty, tq = plane_id(i)
        return pltpu.make_async_remote_copy(
            src_ref=c_ref.at[ty],
            dst_ref=c_all.at[pl.ds(y * 3, 3), pl.ds(pl.multiple_of(q * 16, 16), 16), :],
            send_sem=c_send.at[i], recv_sem=c_recv.at[i],
            device_id=(z * 2 + ty, tq), device_id_type=MESH,
        )

    def s_far(n):
        return pltpu.make_async_remote_copy(
            src_ref=s_ring.at[z], dst_ref=s_ring.at[z],
            send_sem=far_send.at[n], recv_sem=far_recv.at[n],
            device_id=z_id((8, 24)[n]), device_id_type=MESH,
        )

    def s_farther(n):
        half = s_ring.at[block_at((24, 8)[n]), n * 16:n * 16 + 16, :]
        return pltpu.make_async_remote_copy(
            src_ref=half, dst_ref=half,
            send_sem=far_send.at[2 + n], recv_sem=far_recv.at[2 + n],
            device_id=z_id((8, 24)[n]), device_id_type=MESH,
        )

    def hop(k, left, step):
        block = block_at((SEEDS[k] + (step if left else NZ - step)) % NZ)
        slot = k * 7 + (4 if left else 0) + step
        return pltpu.make_async_remote_copy(
            src_ref=s_ring.at[block], dst_ref=s_ring.at[block],
            send_sem=ring_send.at[slot], recv_sem=ring_recv.at[slot],
            device_id=z_id(NZ - 1 if left else 1), device_id_type=MESH,
        )

    def widen(distance):
        block = block_at(distance % NZ)
        rows = s_ring[block].astype(jnp.float32)
        for j in range(4):
            s_wide[j, pl.ds(pl.multiple_of(block * 32, 32), 32), :] = rows[:, j * 128:(j + 1) * 128]

    def hops(k, step):
        return [hop(k, False, step)] + ([hop(k, True, step)] if step < 3 else [])

    def begin(moves):
        for k, step in moves:
            for copy in hops(k, step):
                copy.start()

    def finish(moves):
        for k, step in moves:
            for copy in hops(k, step):
                copy.wait_recv()

    def widen_after(moves):
        for k, step in moves:
            widen(SEEDS[k] - step - 1)
            if step < 3:
                widen(SEEDS[k] + step + 1)

    s_copy.wait()
    for n in range(2):
        s_far(n).start()
    begin([(0, 0)])
    gather_opened(u_one, 0)

    @pl.loop(1, NPLANE)
    def _(i):
        c_copy(i).start()

    widen(0)
    rounds = (
        [(0, 0)],
        [(0, 1)],
        [(0, 2), (1, 0), (2, 0)],
        [(0, 3), (1, 1), (2, 1)],
        [(3, 0), (1, 2), (2, 2)],
        [(3, 1), (1, 3), (2, 3)],
        [(3, 2)],
        [(3, 3)],
    )
    for number, moves in enumerate(rounds):
        if number > 0:
            begin(moves)
            widen_after(rounds[number - 1])
        if number == 2:
            widen(8)
            widen(24)
            gather_passed(u_one, 0)
        if number == 4:
            widen(16)
            gather_closed(u_one, 0)
        finish(moves)
        if number == 1:
            for n in range(2):
                s_far(n).wait_recv()
                s_farther(n).start()
        if number == 3:
            for n in range(2):
                s_farther(n).wait_recv()
    widen_after(rounds[-1])

    @pl.loop(0, 8)
    def _(w):
        for j in range(4):
            s_rows[w, :, j * 128:(j + 1) * 128] = s_wide[j, pl.ds(w, 128, stride=8), :].astype(jnp.bfloat16)

    own_c.wait()

    @pl.loop(1, NPLANE)
    def _(i):
        c_copy(i).wait()

    @pl.loop(0, 6)
    def _(c):
        conduction = c_all[c]
        for w in range(8):
            k_tile[c, :, w * 256:(w + 1) * 256] = lax.dot_general(
                s_rows[w], conduction, (((1,), (1,)), ((), ())), preferred_element_type=jnp.float32
            ).astype(jnp.bfloat16)

    gather_finished(u_one, 0)

    def products(buf, part):
        for block in range(NZ):
            start = (block // 2) * 128 + (block % 2) * 48
            u_wide[start:start + 48, :] = buf[block].astype(jnp.float32).reshape(48, 128)

        for w in range(8):
            u_rows[w * 256:(w + 1) * 256, :] = u_wide[pl.ds(w, 256, stride=8), :].astype(jnp.bfloat16)

        @pl.loop(0, 6)
        def _(c):
            part[c] = jnp.dot(k_tile[c], u_rows[...], preferred_element_type=jnp.float32)

    def sum_copy(part, landing, op, i):
        ty, tq = plane_id(i)
        return pltpu.make_async_remote_copy(
            src_ref=part.at[pl.ds(ty * 3, 3), pl.ds(pl.multiple_of(tq * 8, 8), 8), :],
            dst_ref=landing.at[i],
            send_sem=sum_send.at[op, i], recv_sem=sum_recv.at[op, i],
            device_id=(z * 2 + ty, tq), device_id_type=MESH,
        )

    def reduced(part, landing, op):
        @pl.loop(1, NPLANE)
        def _(i):
            sum_copy(part, landing, op, i).start()

        landing[0] = part[pl.ds(y * 3, 3), pl.ds(pl.multiple_of(q * 8, 8), 8), :]

        @pl.loop(1, NPLANE)
        def _(i):
            sum_copy(part, landing, op, i).wait()

        return jnp.sum(landing[...], axis=0)

    products(u_one, y_part)
    start = u_ref[...].astype(jnp.float32)
    first = ((gaps_ref[...] * start - reduced(y_part, r_one, 0)) / half_width).astype(jnp.bfloat16)
    u_two[z, y] = first
    first_ref[...] = first

    pair_copy(u_two, 1).start()
    gather_opened(u_two, 1)
    gather_passed(u_two, 1)
    gather_closed(u_two, 1)
    gather_finished(u_two, 1)

    products(u_two, y_two)
    second = (gaps_ref[...] * first.astype(jnp.float32) - reduced(y_two, r_two, 1)) / half_width
    filtered_ref[...] = 2.0 * second - start

    for n in range(2):
        s_far(n).wait_send()
        s_farther(n).wait_send()
    for moves in rounds:
        for k, step in moves:
            for copy in hops(k, step):
                copy.wait_send()


def on_device(
    valence_pairs, conduction_pairs, screening, valence_energy, conduction_energy, vectors
):
    gaps = (conduction_energy[:, None] - valence_energy[None, :] - shift_center)[:, :, None]
    gaps = jnp.broadcast_to(gaps, vectors.shape)
    padded = jnp.pad(conduction_pairs, ((0, 0), (0, 4), (0, 0)))
    halves = jnp.transpose(padded.reshape(3, 16, 2, 512), (2, 0, 1, 3))
    in_vmem = pl.BlockSpec(memory_space=pltpu.VMEM)
    bf16, f32 = jnp.bfloat16, jnp.float32
    dma = pltpu.SemaphoreType.DMA
    return pl.pallas_call(
        body,
        out_shape=(
            jax.ShapeDtypeStruct(vectors.shape, bf16),
            jax.ShapeDtypeStruct(vectors.shape, f32),
        ),
        in_specs=[in_vmem, in_vmem, pl.BlockSpec(memory_space=pl.ANY), in_vmem, in_vmem],
        out_specs=(in_vmem, in_vmem),
        scratch_shapes=[
            pltpu.VMEM((1024, 512), bf16),
            pltpu.VMEM((1024, 512), bf16),
            pltpu.VMEM((16, 512), bf16),
            pltpu.VMEM((NZ, 32, 512), bf16),
            pltpu.VMEM((4, 1024, 128), f32),
            pltpu.VMEM((8, 128, 512), bf16),
            pltpu.VMEM((6, 256, 512), bf16),
            pltpu.VMEM((6, 128, 2048), bf16),
            pltpu.VMEM((NZ, 2, 3, 8, 128), bf16),
            pltpu.VMEM((NZ, 2, 3, 8, 128), bf16),
            pltpu.VMEM((2048, 128), f32),
            pltpu.VMEM((2048, 128), bf16),
            pltpu.VMEM((6, 128, 128), f32),
            pltpu.VMEM((6, 128, 128), f32),
            pltpu.VMEM((NPLANE, 3, 8, 128), f32),
            pltpu.VMEM((NPLANE, 3, 8, 128), f32),
            dma((3,)),
            dma((2,)),
            dma((NPLANE,)),
            dma((NPLANE,)),
            dma((4,)),
            dma((4,)),
            dma((28,)),
            dma((28,)),
            dma((2, 33)),
            dma((2, 33)),
            dma((2, NPLANE)),
            dma((2, NPLANE)),
        ],
        compiler_params=pltpu.CompilerParams(collective_id=0, has_side_effects=True),
    )(valence_pairs, halves, screening, gaps, vectors)


def solution(mesh):
    return jax.shard_map(
        on_device,
        mesh=mesh,
        in_specs=(
            P("row", "col", None),
            P("row", "col", None),
            P(),
            P("col"),
            P("row"),
            P("row", "col", None),
        ),
        out_specs=(P("row", "col", None), P("row", "col", None)),
        check_vma=False,
    )
```

time: 163 us -> 130 us (0.80)
  Pallas kernels: 156 us -> 123 us
    pallas_call x1, Pallas kernels: 156 us -> 123 us  [on_device(): pl.pallas_call(body, out_shape=(jax.ShapeDtypeStruct(vectors.shape, bf16)...]
where the time goes in v2:
time: 130 us; the launch traced here: 129 us
  Pallas kernels  123 us (95%)
  local copies, waits for them, and re-layouts  4.82 us (4%)
    pallas_call x1, Pallas kernels, on_device(): pl.pallas_call(body, out_shape=(jax.ShapeDtypeStruct(vectors.shape, bf16)...  123 us

profile of v2, /device:TPU:1, one launch (start us, length us, event | category | flops | bytes accessed | tf_op | source)
XLA Modules:
  0.0 129.4 jit_solution(6345145383860570581)
XLA Ops:
  0.6 0.9 pad.4
  1.5 0.6 copy.11
  2.2 0.7 subtract_add_fusion
  2.9 0.7 broadcast_in_dim.2.gaps_ref
  3.6 123.2 %shard_map.77 = (bf16[3,8,128]{2,1,0:T(8,128)(2,1)}, f32[3,8,128]{2,1,0:T(8,128)}) custom-call(bf16[2,8,1024]{2,1,0:T(8,128)(2,1)} %v_ref.1, bf16[2,3,16,512]{3,2,1,0:T(8,128)(2,1)} %bitcast.7, bf16[1024,1024]{1,0:T(8,128)(2,1)} %screening_ref.1, f32[3,8,128]{2,1,0:T(8,128)} %broadcast_in_dim.2.gaps_ref, bf16[3,8,128]{2,1,0:T(8,128)(2,1)} %u_ref.1), custom_call_target="tpu_custom_call" | custom-call | tf_op jit(solution)/shard_map/pallas_call | solution.py:340
  126.8 1.3 copy.14
  128.1 1.3 %copy.15 = f32[3,8,128]{2,1,0:T(8,128)} copy(f32[3,8,128]{2,1,0:T(8,128)} %get-tuple-element.5) | data formatting | bytes 24576

commit v3 on v2

--- a/solution.py
+++ b/solution.py
@@ -18,9 +18,9 @@
 
 
 def body(
-    v_ref, c_ref, screening_ref, gaps_ref, u_ref,
+    v_ref, c_ref, screening_ref, ve_ref, ce_ref, u_ref,
     first_ref, filtered_ref,
-    screen_own, screen_other, s_pair, s_ring, s_wide, s_rows, c_all, k_tile,
+    gaps, c_half, screen_own, screen_other, s_pair, s_ring, s_wide, s_rows, c_all, k_tile,
     u_one, u_two, u_wide, u_rows, y_part, y_two, r_one, r_two,
     local_sem, v_sem, c_send, c_recv, far_send, far_recv, ring_send, ring_recv,
     gather_send, gather_recv, sum_send, sum_recv,
@@ -58,13 +58,23 @@
 
     screen_copy(1 - y, screen_other, 0).start()
     screen_copy(y, screen_own, 1).start()
+    c_half[...] = jnp.zeros_like(c_half)
+    for half in range(2):
+        for c in range(3):
+            c_half[half, c, 0:12, :] = c_ref[c, :, half * 512:half * 512 + 512]
     own_c = pltpu.make_async_copy(
-        c_ref.at[y],
+        c_half.at[y],
         c_all.at[pl.ds(y * 3, 3), pl.ds(pl.multiple_of(q * 16, 16), 16), :],
         local_sem.at[2],
     )
     own_c.start()
     u_wide[...] = jnp.zeros_like(u_wide)
+    state = lax.broadcasted_iota(jnp.int32, (8, 128), 0)
+    valence = jnp.zeros((8, 128), jnp.float32)
+    for v in range(8):
+        valence = jnp.where(state == v, ve_ref[v], valence)
+    for c in range(3):
+        gaps[c] = ce_ref[c] - valence - shift_center
     u_one[z, y] = u_ref[...]
 
     raw = v_ref[...].astype(jnp.float32).reshape(16, 1024).astype(jnp.bfloat16)
@@ -150,7 +160,7 @@
     def c_copy(i):
         ty, tq = plane_id(i)
         return pltpu.make_async_remote_copy(
-            src_ref=c_ref.at[ty],
+            src_ref=c_half.at[ty],
             dst_ref=c_all.at[pl.ds(y * 3, 3), pl.ds(pl.multiple_of(q * 16, 16), 16), :],
             send_sem=c_send.at[i], recv_sem=c_recv.at[i],
             device_id=(z * 2 + ty, tq), device_id_type=MESH,
@@ -186,30 +196,32 @@
         for j in range(4):
             s_wide[j, pl.ds(pl.multiple_of(block * 32, 32), 32), :] = rows[:, j * 128:(j + 1) * 128]
 
-    def hops(k, step):
-        return [hop(k, False, step)] + ([hop(k, True, step)] if step < 3 else [])
-
-    def begin(moves):
-        for k, step in moves:
-            for copy in hops(k, step):
-                copy.start()
-
-    def finish(moves):
-        for k, step in moves:
-            for copy in hops(k, step):
-                copy.wait_recv()
-
-    def widen_after(moves):
-        for k, step in moves:
-            widen(SEEDS[k] - step - 1)
-            if step < 3:
-                widen(SEEDS[k] + step + 1)
+    def u_hop(k, left, step):
+        block = block_at((SEEDS[k] + (step if left else NZ - step)) % NZ)
+        slot = 5 + k * 7 + (4 if left else 0) + step
+        return pltpu.make_async_remote_copy(
+            src_ref=u_one.at[block], dst_ref=u_one.at[block],
+            send_sem=gather_send.at[0, slot], recv_sem=gather_recv.at[0, slot],
+            device_id=z_id(NZ - 1 if left else 1), device_id_type=MESH,
+        )
+
+    def begin(k, left, step):
+        hop(k, left, step).start()
+        u_hop(k, left, step).start()
+
+    def pass_on(k, left, step):
+        hop(k, left, step).wait_recv()
+        u_hop(k, left, step).wait_recv()
+        if step < (2 if left else 3):
+            begin(k, left, step + 1)
 
     s_copy.wait()
+    pair_copy(u_one, 0).wait()
     for n in range(2):
         s_far(n).start()
-    begin([(0, 0)])
-    gather_opened(u_one, 0)
+        far_copy(u_one, 0, n).start()
+    for left in (False, True):
+        begin(0, left, 0)
 
     @pl.loop(1, NPLANE)
     def _(i):
@@ -221,31 +233,35 @@
         [(0, 1)],
         [(0, 2), (1, 0), (2, 0)],
         [(0, 3), (1, 1), (2, 1)],
-        [(3, 0), (1, 2), (2, 2)],
-        [(3, 1), (1, 3), (2, 3)],
+        [(1, 2), (2, 2), (3, 0)],
+        [(1, 3), (2, 3), (3, 1)],
         [(3, 2)],
         [(3, 3)],
     )
     for number, moves in enumerate(rounds):
-        if number > 0:
-            begin(moves)
-            widen_after(rounds[number - 1])
-        if number == 2:
-            widen(8)
-            widen(24)
-            gather_passed(u_one, 0)
-        if number == 4:
-            widen(16)
-            gather_closed(u_one, 0)
-        finish(moves)
+        for k, step in moves:
+            for left in (False, True)[:2 if step < 3 else 1]:
+                pass_on(k, left, step)
         if number == 1:
             for n in range(2):
                 s_far(n).wait_recv()
                 s_farther(n).start()
+                far_copy(u_one, 0, n).wait_recv()
+                farther_copy(u_one, 0, n).start()
+                for left in (False, True):
+                    begin(1 + n, left, 0)
+                widen((24, 8)[n])
         if number == 3:
             for n in range(2):
                 s_farther(n).wait_recv()
-    widen_after(rounds[-1])
+                farther_copy(u_one, 0, n).wait_recv()
+            for left in (False, True):
+                begin(3, left, 0)
+            widen(16)
+        for k, step in moves:
+            widen(SEEDS[k] - step - 1)
+            if step < 3:
+                widen(SEEDS[k] + step + 1)
 
     @pl.loop(0, 8)
     def _(w):
@@ -266,8 +282,6 @@
                 s_rows[w], conduction, (((1,), (1,)), ((), ())), preferred_element_type=jnp.float32
             ).astype(jnp.bfloat16)
 
-    gather_finished(u_one, 0)
-
     def products(buf, part):
         for block in range(NZ):
             start = (block // 2) * 128 + (block % 2) * 48
@@ -304,7 +318,7 @@
 
     products(u_one, y_part)
     start = u_ref[...].astype(jnp.float32)
-    first = ((gaps_ref[...] * start - reduced(y_part, r_one, 0)) / half_width).astype(jnp.bfloat16)
+    first = ((gaps[...] * start - reduced(y_part, r_one, 0)) / half_width).astype(jnp.bfloat16)
     u_two[z, y] = first
     first_ref[...] = first
 
@@ -315,26 +329,26 @@
     gather_finished(u_two, 1)
 
     products(u_two, y_two)
-    second = (gaps_ref[...] * first.astype(jnp.float32) - reduced(y_two, r_two, 1)) / half_width
+    second = (gaps[...] * first.astype(jnp.float32) - reduced(y_two, r_two, 1)) / half_width
     filtered_ref[...] = 2.0 * second - start
 
     for n in range(2):
         s_far(n).wait_send()
         s_farther(n).wait_send()
+        far_copy(u_one, 0, n).wait_send()
+        farther_copy(u_one, 0, n).wait_send()
     for moves in rounds:
         for k, step in moves:
-            for copy in hops(k, step):
-                copy.wait_send()
+            for left in (False, True)[:2 if step < 3 else 1]:
+                hop(k, left, step).wait_send()
+                u_hop(k, left, step).wait_send()
 
 
 def on_device(
     valence_pairs, conduction_pairs, screening, valence_energy, conduction_energy, vectors
 ):
-    gaps = (conduction_energy[:, None] - valence_energy[None, :] - shift_center)[:, :, None]
-    gaps = jnp.broadcast_to(gaps, vectors.shape)
-    padded = jnp.pad(conduction_pairs, ((0, 0), (0, 4), (0, 0)))
-    halves = jnp.transpose(padded.reshape(3, 16, 2, 512), (2, 0, 1, 3))
     in_vmem = pl.BlockSpec(memory_space=pltpu.VMEM)
+    in_smem = pl.BlockSpec(memory_space=pltpu.SMEM)
     bf16, f32 = jnp.bfloat16, jnp.float32
     dma = pltpu.SemaphoreType.DMA
     return pl.pallas_call(
@@ -343,9 +357,11 @@
             jax.ShapeDtypeStruct(vectors.shape, bf16),
             jax.ShapeDtypeStruct(vectors.shape, f32),
         ),
-        in_specs=[in_vmem, in_vmem, pl.BlockSpec(memory_space=pl.ANY), in_vmem, in_vmem],
+        in_specs=[in_vmem, in_vmem, pl.BlockSpec(memory_space=pl.ANY), in_smem, in_smem, in_vmem],
         out_specs=(in_vmem, in_vmem),
         scratch_shapes=[
+            pltpu.VMEM((3, 8, 128), f32),
+            pltpu.VMEM((2, 3, 16, 512), bf16),
             pltpu.VMEM((1024, 512), bf16),
             pltpu.VMEM((1024, 512), bf16),
             pltpu.VMEM((16, 512), bf16),
@@ -376,7 +392,7 @@
             dma((2, NPLANE)),
         ],
         compiler_params=pltpu.CompilerParams(collective_id=0, has_side_effects=True),
-    )(valence_pairs, halves, screening, gaps, vectors)
+    )(valence_pairs, conduction_pairs, screening, valence_energy, conduction_energy, vectors)
 
 
 def solution(mesh):

time: 130 us -> 121 us (0.931)
  Pallas kernels: 123 us -> 118 us
  local copies, waits for them, and re-layouts: 4.82 us -> 2.59 us
    pallas_call x1, Pallas kernels: 123 us -> 118 us  [on_device(): pl.pallas_call(body, out_shape=(jax.ShapeDtypeStruct(vectors.shape, bf16)...]
where the time goes in v3:
time: 121 us
  Pallas kernels  118 us (98%)
  local copies, waits for them, and re-layouts  2.59 us (2%)
    pallas_call x1, Pallas kernels, on_device(): pl.pallas_call(body, out_shape=(jax.ShapeDtypeStruct(vectors.shape, bf16)...  118 us
    unnamed x2, local copies, waits for them, and re-layouts  2.59 us

profile of v3, /device:TPU:1, one launch (start us, length us, event | category | flops | bytes accessed | tf_op | source)
XLA Modules:
  0.0 121.1 jit_solution(18199279458557083527)
XLA Ops:
  0.6 117.8 %shard_map.77 = (bf16[3,8,128]{2,1,0:T(8,128)(2,1)}, f32[3,8,128]{2,1,0:T(8,128)}) custom-call(bf16[2,8,1024]{2,1,0:T(8,128)(2,1)} %v_ref.1, bf16[3,12,1024]{2,1,0:T(8,128)(2,1)} %c_ref.1, bf16[1024,1024]{1,0:T(8,128)(2,1)} %screening_ref.1, f32[8]{0:T(128)} %ve_ref.1, f32[3]{0:T(128)} %ce_ref.1, bf16[3,8,128]{2,1,0:T(8,128)(2,1)} %u_ref.1), custom_call_target="tpu_custom_call" | custom-call | tf_op jit(solution)/shard_map/pallas_call | solution.py:354
  118.5 1.3 %copy.10 = bf16[3,8,128]{2,1,0:T(8,128)(2,1)} copy(bf16[3,8,128]{2,1,0:T(8,128)(2,1)} %get-tuple-element.4) | data formatting | bytes 12288
  119.8 1.3 %copy.11 = f32[3,8,128]{2,1,0:T(8,128)} copy(f32[3,8,128]{2,1,0:T(8,128)} %get-tuple-element.5) | data formatting | bytes 24576

commit v4 on v3

--- a/solution.py
+++ b/solution.py
@@ -12,7 +12,7 @@
 NQ = 16
 NPLANE = 32
 SEEDS = (0, 24, 8, 16)
-SPREAD = (4, 3, 29, 2, 30, 1, 31)
+SPREAD = (4, 3, -3, 2, -2, 1, -1)
 GREETED = (1, 2, 3, 4, 8, 24, 28, 29, 30, 31)
 MESH = pl.DeviceIdType.MESH
 
@@ -30,16 +30,17 @@
     z = row // 2
     y = row % 2
     me = y * NQ + q
+    side = 1 - 2 * (q % 2)
 
     def plane_id(i):
         p = (me + i) % NPLANE
         return p // NQ, p % NQ
 
     def z_id(distance):
-        return (((z + distance) % NZ) * 2 + y, q)
+        return (((z + distance + NZ) % NZ) * 2 + y, q)
 
     def block_at(distance):
-        return (z + distance) % NZ
+        return (z + distance + 2 * NZ) % NZ
 
     barrier = pltpu.get_barrier_semaphore()
 
@@ -122,7 +123,7 @@
         return pltpu.make_async_remote_copy(
             src_ref=buf.at[block], dst_ref=buf.at[block],
             send_sem=gather_send.at[op, slot], recv_sem=gather_recv.at[op, slot],
-            device_id=z_id(SPREAD[n]), device_id_type=MESH,
+            device_id=z_id(side * SPREAD[n]), device_id_type=MESH,
         )
 
     def spread(buf, op, k):
@@ -182,27 +183,27 @@
         )
 
     def hop(k, left, step):
-        block = block_at((SEEDS[k] + (step if left else NZ - step)) % NZ)
+        block = block_at(SEEDS[k] + side * (step if left else -step))
         slot = k * 7 + (4 if left else 0) + step
         return pltpu.make_async_remote_copy(
             src_ref=s_ring.at[block], dst_ref=s_ring.at[block],
             send_sem=ring_send.at[slot], recv_sem=ring_recv.at[slot],
-            device_id=z_id(NZ - 1 if left else 1), device_id_type=MESH,
+            device_id=z_id(side * (-1 if left else 1)), device_id_type=MESH,
         )
 
     def widen(distance):
-        block = block_at(distance % NZ)
+        block = block_at(distance)
         rows = s_ring[block].astype(jnp.float32)
         for j in range(4):
             s_wide[j, pl.ds(pl.multiple_of(block * 32, 32), 32), :] = rows[:, j * 128:(j + 1) * 128]
 
     def u_hop(k, left, step):
-        block = block_at((SEEDS[k] + (step if left else NZ - step)) % NZ)
+        block = block_at(SEEDS[k] + side * (step if left else -step))
         slot = 5 + k * 7 + (4 if left else 0) + step
         return pltpu.make_async_remote_copy(
             src_ref=u_one.at[block], dst_ref=u_one.at[block],
             send_sem=gather_send.at[0, slot], recv_sem=gather_recv.at[0, slot],
-            device_id=z_id(NZ - 1 if left else 1), device_id_type=MESH,
+            device_id=z_id(side * (-1 if left else 1)), device_id_type=MESH,
         )
 
     def begin(k, left, step):
@@ -259,9 +260,9 @@
                 begin(3, left, 0)
             widen(16)
         for k, step in moves:
-            widen(SEEDS[k] - step - 1)
+            widen(SEEDS[k] - side * (step + 1))
             if step < 3:
-                widen(SEEDS[k] + step + 1)
+                widen(SEEDS[k] + side * (step + 1))
 
     @pl.loop(0, 8)
     def _(w):

time: 121 us -> 121 us (level)
  no operation moved by 1% of the time
where the time goes in v4:
time: 121 us; the launch traced here: 120 us
  Pallas kernels  117 us (97%)
  local copies, waits for them, and re-layouts  2.59 us (2%)
    pallas_call x1, Pallas kernels, on_device(): pl.pallas_call(body, out_shape=(jax.ShapeDtypeStruct(vectors.shape, bf16)...  117 us
    unnamed x2, local copies, waits for them, and re-layouts  2.59 us

profile of v4, /device:TPU:1, one launch (start us, length us, event | category | flops | bytes accessed | tf_op | source)
XLA Modules:
  0.0 120.3 jit_solution(16600232137100177702)
XLA Ops:
  0.6 117.1 %shard_map.77 = (bf16[3,8,128]{2,1,0:T(8,128)(2,1)}, f32[3,8,128]{2,1,0:T(8,128)}) custom-call(bf16[2,8,1024]{2,1,0:T(8,128)(2,1)} %v_ref.1, bf16[3,12,1024]{2,1,0:T(8,128)(2,1)} %c_ref.1, bf16[1024,1024]{1,0:T(8,128)(2,1)} %screening_ref.1, f32[8]{0:T(128)} %ve_ref.1, f32[3]{0:T(128)} %ce_ref.1, bf16[3,8,128]{2,1,0:T(8,128)(2,1)} %u_ref.1), custom_call_target="tpu_custom_call" | custom-call | tf_op jit(solution)/shard_map/pallas_call | solution.py:355
  117.7 1.3 %copy.10 = bf16[3,8,128]{2,1,0:T(8,128)(2,1)} copy(bf16[3,8,128]{2,1,0:T(8,128)(2,1)} %get-tuple-element.4) | data formatting | bytes 12288
  119.0 1.3 %copy.11 = f32[3,8,128]{2,1,0:T(8,128)} copy(f32[3,8,128]{2,1,0:T(8,128)} %get-tuple-element.5) | data formatting | bytes 24576
